TPU v7x, 32 devices: a whole 2x2x4 slice. The times are simulated.
32 devices in a mesh: pair: 2 (over x), grow: 4 (over y, core), gcol: 4 (over z).
Axes of the slice: x: 2, y: 2, z: 4, core: 2. Of those that a mesh axis runs over, the one named last changes fastest.
Arguments:
- core_matrix: bfloat16 [12288, 12288], P('grow', 'gcol'), may hold values from -0.00048828125 to 0.00048828125
- pair_panels: bfloat16 [12, 32, 12288], P('pair', None, ('grow', 'gcol')), may hold values from -6 to 6
- amplitudes: bfloat16 [12, 32, 32], P('pair'), may hold values from -0.1875 to 0.1875
- pair_widths: int32 [12], P('pair'), may hold values from 8 to 32
- batch_plan: int32 [12], P('pair'), may hold values from 0 to 11, each once
Outputs:
- residual: float32 [12, 1024], P('pair', ('grow', 'gcol'))
Inputs may be any that keep to these rules, and one draw needn't show every extreme that they name: batch_plan names every pair exactly once.
All inputs are finite; a program needn't handle non-finite values.
Results may differ from a plain program's by a relative error of at most 0.015.
Values may be sent and summed in bfloat16 or wider, within the bound.
A program may use at most 64 MiB of HBM per device.

v0:
```python
import jax
import jax.numpy as jnp
from jax import lax
from jax.sharding import PartitionSpec as P


def local(core_matrix, pair_panels, amplitudes, pair_widths, batch_plan):
    depth = amplitudes.shape[1]
    live = (
        lax.broadcasted_iota(jnp.int32, (pair_widths.shape[0], depth), 1) < pair_widths[:, None]
    ).astype(jnp.bfloat16)
    masked = amplitudes * live[:, :, None] * live[:, None, :]
    row_index = lax.axis_index("grow")
    col_index = lax.axis_index("gcol")
    row_len = core_matrix.shape[0]
    col_len = core_matrix.shape[1]
    gathered = lax.all_gather(pair_panels, ("grow", "gcol"), axis=2, tiled=True)
    left = lax.dynamic_slice_in_dim(gathered, row_index * row_len, row_len, 2)
    right = lax.dynamic_slice_in_dim(gathered, col_index * col_len, col_len, 2)

    def slot_term(items):
        left_panel, right_panel, amps, mask = items
        projected = jnp.dot(amps, right_panel, preferred_element_type=jnp.float32).astype(
            jnp.bfloat16
        )
        coupled = lax.dot_general(
            left_panel, projected, (((0,), (0,)), ((), ())), preferred_element_type=jnp.float32
        ).astype(jnp.bfloat16)
        coupled = lax.optimization_barrier(coupled)
        weighted = (core_matrix.astype(jnp.float32) * coupled.astype(jnp.float32)).astype(
            jnp.bfloat16
        )
        back = lax.dot_general(
            weighted, right_panel, (((1,), (1,)), ((), ())), preferred_element_type=jnp.float32
        ).astype(jnp.bfloat16)
        partial_sum = jnp.dot(left_panel, back, preferred_element_type=jnp.float32)
        keep = mask.astype(jnp.float32)
        return (partial_sum * keep[:, None] * keep[None, :]).reshape(depth * depth)

    terms = lax.map(slot_term, (left, right, masked, live))
    total = lax.psum(terms, ("grow", "gcol"))
    share = terms.shape[1] // lax.axis_size(("grow", "gcol"))
    reduced = lax.dynamic_slice_in_dim(total, lax.axis_index(("grow", "gcol")) * share, share, 1)
    every_row = lax.all_gather(reduced, "pair", axis=0, tiled=True)
    return jnp.take(every_row, batch_plan, axis=0)


def solution(mesh):
    in_specs = (
        P("grow", "gcol"),
        P("pair", None, ("grow", "gcol")),
        P("pair", None, None),
        P("pair"),
        P("pair"),
    )
    out_specs = P("pair", ("grow", "gcol"))
    return jax.shard_map(local, mesh=mesh, in_specs=in_specs, out_specs=out_specs, check_vma=False)
```

profile of v0, /device:TPU:0, one launch (start us, length us, event | category | flops | bytes accessed | tf_op | source)
XLA Modules:
  0.0 285.3 jit_solution(8804718714653839679)
XLA Ops:
  6.5 0.0 all-gather.3.cloned.1.call-start
  6.5 0.7 all-gather.3.cloned.1.call-update
  7.3 0.7 compare_select_fusion
  8.0 0.7 compare_and_fusion
  8.6 0.7 fusion.27
  9.3 0.9 multiply_multiply_fusion
  10.2 55.5 %all-gather.3.cloned.1.call-done = bf16[6,32,12288]{2,1,0:T(8,128)(2,1)} async-done(((bf16[6,32,768]{2,1,0:T(8,128)(2,1)}), bf16[6,32,12288]{2,1,0:T(8,128)(2,1)}) %all-gather.3.cloned.1.call-update) | async-done | bytes 4718608 | tf_op jit(solution)/shard_map/all_gather | solution.py:17
  65.8 1.9 constant_dynamic-slice_fusion.1
  67.6 145.8 %while.10 = (s32[]{:T(128)}, f32[6,1024]{1,0:T(8,128)S(1)}, bf16[6,32,3072]{2,1,0:T(8,128)(2,1)S(1)}, bf16[3072,3072]{1,0:T(8,128)(2,1)}, bf16[6,32,32]{2,1,0:T(...) while((s32[]{:T(128)}, f32[6,1024]{1,0:T(8,128)S(1)}, ...), condition=%wide.region_1.2_spmd, body=%wide.region_0.1_spmd.sunk | while | flops 1267927040 | bytes 57442084 | solution.py:40
  67.6 9.3 %convolution_convert_fusion.3 = bf16[3072,3072]{1,0:T(8,128)(2,1)} fusion(bf16[6,32,3072]{2,1,0:T(8,128)(2,1)S(1)} %get-tuple-element.125, s32[]{:T(128)} %get-tuple-element.111, bf16[6,32,3072]{2,1,0:T(8,128)(2,1)S(1)} %get-tuple-element.122, bf16[6,32,32]{2,1,0:T(8,128)(2,1)S(1)} %get-tuple-element.124), kind=kOutput, calls=%fused_computation.3.clone.1 | convolution fusion | flops 619806720 | bytes 19277312 | tf_op jit(solution)/shard_map/while/body/eval_jaxpr/dot_general | solution.py:26
  77.0 14.8 %fusion.41 = f32[32,32]{1,0:T(8,128)S(1)} fusion(bf16[3072,3072]{1,0:T(8,128)(2,1)} %convolution_convert_fusion.3, bf16[3072,3072]{1,0:T(8,128)(2,1)} %get-tuple-element.123, bf16[6,32,3072]{2,1,0:T(8,128)(2,1)S(1)} %get-tuple-element.125, s32[]{:T(128)} %get-tuple-element.111, bf16[6,32,3072]{2,1,0:T(8,128)(2,1)S(1)} %get-tuple-element.122, ...), kind=kOutput, calls=%fused_computation.8.clone.1 | convolution fusion | flops 648120320 | bytes 38148096 | tf_op jit(solution)/shard_map/while/body/eval_jaxpr/dot_general | solution.py:36
  91.8 0.1 broadcast_in_dim.31
  91.8 0.1 dynamic_update_slice.5
  91.9 9.3 %convolution_convert_fusion.3 = bf16[3072,3072]{1,0:T(8,128)(2,1)} fusion(bf16[6,32,3072]{2,1,0:T(8,128)(2,1)S(1)} %get-tuple-element.125, s32[]{:T(128)} %get-tuple-element.111, bf16[6,32,3072]{2,1,0:T(8,128)(2,1)S(1)} %get-tuple-element.122, bf16[6,32,32]{2,1,0:T(8,128)(2,1)S(1)} %get-tuple-element.124), kind=kOutput, calls=%fused_computation.3.clone.1 | convolution fusion | flops 619806720 | bytes 19277312 | tf_op jit(solution)/shard_map/while/body/eval_jaxpr/dot_general | solution.py:26
  101.3 14.8 %fusion.41 = f32[32,32]{1,0:T(8,128)S(1)} fusion(bf16[3072,3072]{1,0:T(8,128)(2,1)} %convolution_convert_fusion.3, bf16[3072,3072]{1,0:T(8,128)(2,1)} %get-tuple-element.123, bf16[6,32,3072]{2,1,0:T(8,128)(2,1)S(1)} %get-tuple-element.125, s32[]{:T(128)} %get-tuple-element.111, bf16[6,32,3072]{2,1,0:T(8,128)(2,1)S(1)} %get-tuple-element.122, ...), kind=kOutput, calls=%fused_computation.8.clone.1 | convolution fusion | flops 648120320 | bytes 38148096 | tf_op jit(solution)/shard_map/while/body/eval_jaxpr/dot_general | solution.py:36
  116.1 0.1 broadcast_in_dim.31
  116.1 0.1 dynamic_update_slice.5
  116.2 9.3 %convolution_convert_fusion.3 = bf16[3072,3072]{1,0:T(8,128)(2,1)} fusion(bf16[6,32,3072]{2,1,0:T(8,128)(2,1)S(1)} %get-tuple-element.125, s32[]{:T(128)} %get-tuple-element.111, bf16[6,32,3072]{2,1,0:T(8,128)(2,1)S(1)} %get-tuple-element.122, bf16[6,32,32]{2,1,0:T(8,128)(2,1)S(1)} %get-tuple-element.124), kind=kOutput, calls=%fused_computation.3.clone.1 | convolution fusion | flops 619806720 | bytes 19277312 | tf_op jit(solution)/shard_map/while/body/eval_jaxpr/dot_general | solution.py:26
  125.6 14.8 %fusion.41 = f32[32,32]{1,0:T(8,128)S(1)} fusion(bf16[3072,3072]{1,0:T(8,128)(2,1)} %convolution_convert_fusion.3, bf16[3072,3072]{1,0:T(8,128)(2,1)} %get-tuple-element.123, bf16[6,32,3072]{2,1,0:T(8,128)(2,1)S(1)} %get-tuple-element.125, s32[]{:T(128)} %get-tuple-element.111, bf16[6,32,3072]{2,1,0:T(8,128)(2,1)S(1)} %get-tuple-element.122, ...), kind=kOutput, calls=%fused_computation.8.clone.1 | convolution fusion | flops 648120320 | bytes 38148096 | tf_op jit(solution)/shard_map/while/body/eval_jaxpr/dot_general | solution.py:36
  140.3 0.1 broadcast_in_dim.31
  140.4 0.1 dynamic_update_slice.5
  140.5 9.3 %convolution_convert_fusion.3 = bf16[3072,3072]{1,0:T(8,128)(2,1)} fusion(bf16[6,32,3072]{2,1,0:T(8,128)(2,1)S(1)} %get-tuple-element.125, s32[]{:T(128)} %get-tuple-element.111, bf16[6,32,3072]{2,1,0:T(8,128)(2,1)S(1)} %get-tuple-element.122, bf16[6,32,32]{2,1,0:T(8,128)(2,1)S(1)} %get-tuple-element.124), kind=kOutput, calls=%fused_computation.3.clone.1 | convolution fusion | flops 619806720 | bytes 19277312 | tf_op jit(solution)/shard_map/while/body/eval_jaxpr/dot_general | solution.py:26
  149.9 14.8 %fusion.41 = f32[32,32]{1,0:T(8,128)S(1)} fusion(bf16[3072,3072]{1,0:T(8,128)(2,1)} %convolution_convert_fusion.3, bf16[3072,3072]{1,0:T(8,128)(2,1)} %get-tuple-element.123, bf16[6,32,3072]{2,1,0:T(8,128)(2,1)S(1)} %get-tuple-element.125, s32[]{:T(128)} %get-tuple-element.111, bf16[6,32,3072]{2,1,0:T(8,128)(2,1)S(1)} %get-tuple-element.122, ...), kind=kOutput, calls=%fused_computation.8.clone.1 | convolution fusion | flops 648120320 | bytes 38148096 | tf_op jit(solution)/shard_map/while/body/eval_jaxpr/dot_general | solution.py:36
  164.6 0.1 broadcast_in_dim.31
  164.7 0.1 dynamic_update_slice.5
  164.8 9.3 %convolution_convert_fusion.3 = bf16[3072,3072]{1,0:T(8,128)(2,1)} fusion(bf16[6,32,3072]{2,1,0:T(8,128)(2,1)S(1)} %get-tuple-element.125, s32[]{:T(128)} %get-tuple-element.111, bf16[6,32,3072]{2,1,0:T(8,128)(2,1)S(1)} %get-tuple-element.122, bf16[6,32,32]{2,1,0:T(8,128)(2,1)S(1)} %get-tuple-element.124), kind=kOutput, calls=%fused_computation.3.clone.1 | convolution fusion | flops 619806720 | bytes 19277312 | tf_op jit(solution)/shard_map/while/body/eval_jaxpr/dot_general | solution.py:26
  174.2 14.8 %fusion.41 = f32[32,32]{1,0:T(8,128)S(1)} fusion(bf16[3072,3072]{1,0:T(8,128)(2,1)} %convolution_convert_fusion.3, bf16[3072,3072]{1,0:T(8,128)(2,1)} %get-tuple-element.123, bf16[6,32,3072]{2,1,0:T(8,128)(2,1)S(1)} %get-tuple-element.125, s32[]{:T(128)} %get-tuple-element.111, bf16[6,32,3072]{2,1,0:T(8,128)(2,1)S(1)} %get-tuple-element.122, ...), kind=kOutput, calls=%fused_computation.8.clone.1 | convolution fusion | flops 648120320 | bytes 38148096 | tf_op jit(solution)/shard_map/while/body/eval_jaxpr/dot_general | solution.py:36
  188.9 0.1 broadcast_in_dim.31
  189.0 0.1 dynamic_update_slice.5
  189.1 9.3 %convolution_convert_fusion.3 = bf16[3072,3072]{1,0:T(8,128)(2,1)} fusion(bf16[6,32,3072]{2,1,0:T(8,128)(2,1)S(1)} %get-tuple-element.125, s32[]{:T(128)} %get-tuple-element.111, bf16[6,32,3072]{2,1,0:T(8,128)(2,1)S(1)} %get-tuple-element.122, bf16[6,32,32]{2,1,0:T(8,128)(2,1)S(1)} %get-tuple-element.124), kind=kOutput, calls=%fused_computation.3.clone.1 | convolution fusion | flops 619806720 | bytes 19277312 | tf_op jit(solution)/shard_map/while/body/eval_jaxpr/dot_general | solution.py:26
  198.5 14.8 %fusion.41 = f32[32,32]{1,0:T(8,128)S(1)} fusion(bf16[3072,3072]{1,0:T(8,128)(2,1)} %convolution_convert_fusion.3, bf16[3072,3072]{1,0:T(8,128)(2,1)} %get-tuple-element.123, bf16[6,32,3072]{2,1,0:T(8,128)(2,1)S(1)} %get-tuple-element.125, s32[]{:T(128)} %get-tuple-element.111, bf16[6,32,3072]{2,1,0:T(8,128)(2,1)S(1)} %get-tuple-element.122, ...), kind=kOutput, calls=%fused_computation.8.clone.1 | convolution fusion | flops 648120320 | bytes 38148096 | tf_op jit(solution)/shard_map/while/body/eval_jaxpr/dot_general | solution.py:36
  213.2 0.1 broadcast_in_dim.31
  213.3 0.1 dynamic_update_slice.5
  213.4 59.4 %psum.7 = f32[6,1024]{1,0:T(8,128)S(1)} all-reduce(f32[6,1024]{1,0:T(8,128)S(1)} %get-tuple-element.42), channel_id=1, replica_groups=mesh['pair'=2,'grow'=4,'gcol'=4] {'grow','gcol'}, use_global_device_ids=true, to_apply=%region_2.3 | all-reduce | flops 6144 | bytes 49152 | tf_op jit(solution)/shard_map/psum | solution.py:41
  272.8 0.1 dynamic-slice_bitcast_fusion
  272.9 4.3 %all-gather = f32[2,6,64]{2,1,0:T(8,128)S(1)} all-gather(f32[1,6,64]{2,1,0:T(8,128)S(1)} %dynamic-slice_bitcast_fusion), channel_id=1, replica_groups=mesh['pair'=2,'grow'=4,'gcol'=4] {'pair'}, dimensions={0}, use_global_device_ids=true | all-gather | bytes 4608 | tf_op jit(solution)/shard_map/all_gather | solution.py:44
  277.2 0.6 gather_fusion
  277.8 0.7 broadcast_select_fusion
  (9 shorter events, 0.0 us)
Async XLA Ops:
  6.5 59.2 %all-gather.3.cloned.1.call-start = ((), (), s32[]{:S(2)}) async-start(), calls=%async_computation | async-start | bytes 5013504 | tf_op jit(solution)/shard_map/all_gather | solution.py:17
Sparse Core Ops, SparseCore 0:
  9.5 56.1 all-gather.2
where the time goes:
time: 286 us; the launch traced here: 285 us
  matrix products  145 us (51%)
  blocking collectives  63.7 us (22%)
  waiting for transfers between devices  56.2 us (20%)
  between operations  13.4 us (5%)
  other arithmetic  3.64 us (1%)
  local copies, waits for them, and re-layouts  3.44 us (1%)
    dot_general x6, matrix products, slot_term(): partial_sum = jnp.dot(left_panel, back, preferred_element_type=jnp.float32)  88.5 us
    psum x1, blocking collectives, local(): total = lax.psum(terms, ('grow', 'gcol'))  59.4 us
    dot_general x6, matrix products, slot_term(): lax.dot_general(left_panel, projected, (((0,), (0,)), ((), ())), preferre...  56.1 us
    all_gather x1, waiting for transfers between devices, local(): gathered = lax.all_gather(pair_panels, ('grow', 'gcol'), axis=2, tiled=True)  55.5 us
  transfers between devices with their start and end apart: 1, of which 1 were waited for; matrix products, arithmetic and copies ran while one was open for 1% of the time, Pallas kernels for 0%

commit v1 on v0

--- a/solution.py
+++ b/solution.py
@@ -38,7 +38,7 @@
         return (partial_sum * keep[:, None] * keep[None, :]).reshape(depth * depth)
 
     terms = lax.map(slot_term, (left, right, masked, live))
-    total = lax.psum(terms, ("grow", "gcol"))
+    total = lax.psum(lax.psum(terms, "grow"), "gcol")
     share = terms.shape[1] // lax.axis_size(("grow", "gcol"))
     reduced = lax.dynamic_slice_in_dim(total, lax.axis_index(("grow", "gcol")) * share, share, 1)
     every_row = lax.all_gather(reduced, "pair", axis=0, tiled=True)

time: 286 us -> 254 us (0.89)
  blocking collectives: 63.7 us -> 32.2 us
    psum x1 -> x2, blocking collectives: 59.4 us -> 27.8 us  [local(): total = lax.psum(lax.psum(terms, 'grow'), 'gcol')]
where the time goes in v1:
time: 254 us
  matrix products  145 us (57%)
  waiting for transfers between devices  56.2 us (22%)
  blocking collectives  32.2 us (13%)
  between operations  13.5 us (5%)
  other arithmetic  3.64 us (1%)
  local copies, waits for them, and re-layouts  3.51 us (1%)
    dot_general x6, matrix products, slot_term(): partial_sum = jnp.dot(left_panel, back, preferred_element_type=jnp.float32)  88.5 us
    dot_general x6, matrix products, slot_term(): lax.dot_general(left_panel, projected, (((0,), (0,)), ((), ())), preferre...  56.1 us
    all_gather x1, waiting for transfers between devices, local(): gathered = lax.all_gather(pair_panels, ('grow', 'gcol'), axis=2, tiled=True)  55.5 us
    psum x2, blocking collectives, local(): total = lax.psum(lax.psum(terms, 'grow'), 'gcol')  27.8 us
  transfers between devices with their start and end apart: 1, of which 1 were waited for; matrix products, arithmetic and copies ran while one was open for 1% of the time, Pallas kernels for 0%

profile of v1, /device:TPU:0, one launch (start us, length us, event | category | flops | bytes accessed | tf_op | source)
XLA Modules:
  0.0 253.8 jit_solution(17306189522465135303)
XLA Ops:
  6.5 0.0 all-gather.3.cloned.1.call-start
  6.5 0.7 all-gather.3.cloned.1.call-update
  7.3 0.7 compare_select_fusion
  8.0 0.7 compare_and_fusion
  8.6 0.7 fusion.27
  9.3 0.9 multiply_multiply_fusion
  10.2 55.5 %all-gather.3.cloned.1.call-done = bf16[6,32,12288]{2,1,0:T(8,128)(2,1)} async-done(((bf16[6,32,768]{2,1,0:T(8,128)(2,1)}), bf16[6,32,12288]{2,1,0:T(8,128)(2,1)}) %all-gather.3.cloned.1.call-update) | async-done | bytes 4718608 | tf_op jit(solution)/shard_map/all_gather | solution.py:17
  65.8 1.9 constant_dynamic-slice_fusion.1
  67.7 145.8 %while.10 = (s32[]{:T(128)}, f32[6,1024]{1,0:T(8,128)S(1)}, bf16[6,32,3072]{2,1,0:T(8,128)(2,1)S(1)}, bf16[3072,3072]{1,0:T(8,128)(2,1)}, bf16[6,32,32]{2,1,0:T(...) while((s32[]{:T(128)}, f32[6,1024]{1,0:T(8,128)S(1)}, ...), condition=%wide.region_1.2_spmd, body=%wide.region_0.1_spmd.sunk | while | flops 1267927040 | bytes 57442084 | solution.py:40
  67.7 9.4 %convolution_convert_fusion.3 = bf16[3072,3072]{1,0:T(8,128)(2,1)} fusion(bf16[6,32,3072]{2,1,0:T(8,128)(2,1)S(1)} %get-tuple-element.125, s32[]{:T(128)} %get-tuple-element.111, bf16[6,32,3072]{2,1,0:T(8,128)(2,1)S(1)} %get-tuple-element.122, bf16[6,32,32]{2,1,0:T(8,128)(2,1)S(1)} %get-tuple-element.124), kind=kOutput, calls=%fused_computation.3.clone.1 | convolution fusion | flops 619806720 | bytes 19277312 | tf_op jit(solution)/shard_map/while/body/eval_jaxpr/dot_general | solution.py:26
  77.1 14.8 %fusion.41 = f32[32,32]{1,0:T(8,128)S(1)} fusion(bf16[3072,3072]{1,0:T(8,128)(2,1)} %convolution_convert_fusion.3, bf16[3072,3072]{1,0:T(8,128)(2,1)} %get-tuple-element.123, bf16[6,32,3072]{2,1,0:T(8,128)(2,1)S(1)} %get-tuple-element.125, s32[]{:T(128)} %get-tuple-element.111, bf16[6,32,3072]{2,1,0:T(8,128)(2,1)S(1)} %get-tuple-element.122, ...), kind=kOutput, calls=%fused_computation.8.clone.1 | convolution fusion | flops 648120320 | bytes 38148096 | tf_op jit(solution)/shard_map/while/body/eval_jaxpr/dot_general | solution.py:36
  91.8 0.1 broadcast_in_dim.31
  91.9 0.1 dynamic_update_slice.5
  92.0 9.4 %convolution_convert_fusion.3 = bf16[3072,3072]{1,0:T(8,128)(2,1)} fusion(bf16[6,32,3072]{2,1,0:T(8,128)(2,1)S(1)} %get-tuple-element.125, s32[]{:T(128)} %get-tuple-element.111, bf16[6,32,3072]{2,1,0:T(8,128)(2,1)S(1)} %get-tuple-element.122, bf16[6,32,32]{2,1,0:T(8,128)(2,1)S(1)} %get-tuple-element.124), kind=kOutput, calls=%fused_computation.3.clone.1 | convolution fusion | flops 619806720 | bytes 19277312 | tf_op jit(solution)/shard_map/while/body/eval_jaxpr/dot_general | solution.py:26
  101.4 14.8 %fusion.41 = f32[32,32]{1,0:T(8,128)S(1)} fusion(bf16[3072,3072]{1,0:T(8,128)(2,1)} %convolution_convert_fusion.3, bf16[3072,3072]{1,0:T(8,128)(2,1)} %get-tuple-element.123, bf16[6,32,3072]{2,1,0:T(8,128)(2,1)S(1)} %get-tuple-element.125, s32[]{:T(128)} %get-tuple-element.111, bf16[6,32,3072]{2,1,0:T(8,128)(2,1)S(1)} %get-tuple-element.122, ...), kind=kOutput, calls=%fused_computation.8.clone.1 | convolution fusion | flops 648120320 | bytes 38148096 | tf_op jit(solution)/shard_map/while/body/eval_jaxpr/dot_general | solution.py:36
  116.1 0.1 broadcast_in_dim.31
  116.2 0.1 dynamic_update_slice.5
  116.3 9.4 %convolution_convert_fusion.3 = bf16[3072,3072]{1,0:T(8,128)(2,1)} fusion(bf16[6,32,3072]{2,1,0:T(8,128)(2,1)S(1)} %get-tuple-element.125, s32[]{:T(128)} %get-tuple-element.111, bf16[6,32,3072]{2,1,0:T(8,128)(2,1)S(1)} %get-tuple-element.122, bf16[6,32,32]{2,1,0:T(8,128)(2,1)S(1)} %get-tuple-element.124), kind=kOutput, calls=%fused_computation.3.clone.1 | convolution fusion | flops 619806720 | bytes 19277312 | tf_op jit(solution)/shard_map/while/body/eval_jaxpr/dot_general | solution.py:26
  125.7 14.8 %fusion.41 = f32[32,32]{1,0:T(8,128)S(1)} fusion(bf16[3072,3072]{1,0:T(8,128)(2,1)} %convolution_convert_fusion.3, bf16[3072,3072]{1,0:T(8,128)(2,1)} %get-tuple-element.123, bf16[6,32,3072]{2,1,0:T(8,128)(2,1)S(1)} %get-tuple-element.125, s32[]{:T(128)} %get-tuple-element.111, bf16[6,32,3072]{2,1,0:T(8,128)(2,1)S(1)} %get-tuple-element.122, ...), kind=kOutput, calls=%fused_computation.8.clone.1 | convolution fusion | flops 648120320 | bytes 38148096 | tf_op jit(solution)/shard_map/while/body/eval_jaxpr/dot_general | solution.py:36
  140.4 0.1 broadcast_in_dim.31
  140.5 0.1 dynamic_update_slice.5
  140.6 9.4 %convolution_convert_fusion.3 = bf16[3072,3072]{1,0:T(8,128)(2,1)} fusion(bf16[6,32,3072]{2,1,0:T(8,128)(2,1)S(1)} %get-tuple-element.125, s32[]{:T(128)} %get-tuple-element.111, bf16[6,32,3072]{2,1,0:T(8,128)(2,1)S(1)} %get-tuple-element.122, bf16[6,32,32]{2,1,0:T(8,128)(2,1)S(1)} %get-tuple-element.124), kind=kOutput, calls=%fused_computation.3.clone.1 | convolution fusion | flops 619806720 | bytes 19277312 | tf_op jit(solution)/shard_map/while/body/eval_jaxpr/dot_general | solution.py:26
  150.0 14.8 %fusion.41 = f32[32,32]{1,0:T(8,128)S(1)} fusion(bf16[3072,3072]{1,0:T(8,128)(2,1)} %convolution_convert_fusion.3, bf16[3072,3072]{1,0:T(8,128)(2,1)} %get-tuple-element.123, bf16[6,32,3072]{2,1,0:T(8,128)(2,1)S(1)} %get-tuple-element.125, s32[]{:T(128)} %get-tuple-element.111, bf16[6,32,3072]{2,1,0:T(8,128)(2,1)S(1)} %get-tuple-element.122, ...), kind=kOutput, calls=%fused_computation.8.clone.1 | convolution fusion | flops 648120320 | bytes 38148096 | tf_op jit(solution)/shard_map/while/body/eval_jaxpr/dot_general | solution.py:36
  164.7 0.1 broadcast_in_dim.31
  164.8 0.1 dynamic_update_slice.5
  164.9 9.4 %convolution_convert_fusion.3 = bf16[3072,3072]{1,0:T(8,128)(2,1)} fusion(bf16[6,32,3072]{2,1,0:T(8,128)(2,1)S(1)} %get-tuple-element.125, s32[]{:T(128)} %get-tuple-element.111, bf16[6,32,3072]{2,1,0:T(8,128)(2,1)S(1)} %get-tuple-element.122, bf16[6,32,32]{2,1,0:T(8,128)(2,1)S(1)} %get-tuple-element.124), kind=kOutput, calls=%fused_computation.3.clone.1 | convolution fusion | flops 619806720 | bytes 19277312 | tf_op jit(solution)/shard_map/while/body/eval_jaxpr/dot_general | solution.py:26
  174.3 14.8 %fusion.41 = f32[32,32]{1,0:T(8,128)S(1)} fusion(bf16[3072,3072]{1,0:T(8,128)(2,1)} %convolution_convert_fusion.3, bf16[3072,3072]{1,0:T(8,128)(2,1)} %get-tuple-element.123, bf16[6,32,3072]{2,1,0:T(8,128)(2,1)S(1)} %get-tuple-element.125, s32[]{:T(128)} %get-tuple-element.111, bf16[6,32,3072]{2,1,0:T(8,128)(2,1)S(1)} %get-tuple-element.122, ...), kind=kOutput, calls=%fused_computation.8.clone.1 | convolution fusion | flops 648120320 | bytes 38148096 | tf_op jit(solution)/shard_map/while/body/eval_jaxpr/dot_general | solution.py:36
  189.0 0.1 broadcast_in_dim.31
  189.1 0.1 dynamic_update_slice.5
  189.2 9.4 %convolution_convert_fusion.3 = bf16[3072,3072]{1,0:T(8,128)(2,1)} fusion(bf16[6,32,3072]{2,1,0:T(8,128)(2,1)S(1)} %get-tuple-element.125, s32[]{:T(128)} %get-tuple-element.111, bf16[6,32,3072]{2,1,0:T(8,128)(2,1)S(1)} %get-tuple-element.122, bf16[6,32,32]{2,1,0:T(8,128)(2,1)S(1)} %get-tuple-element.124), kind=kOutput, calls=%fused_computation.3.clone.1 | convolution fusion | flops 619806720 | bytes 19277312 | tf_op jit(solution)/shard_map/while/body/eval_jaxpr/dot_general | solution.py:26
  198.6 14.8 %fusion.41 = f32[32,32]{1,0:T(8,128)S(1)} fusion(bf16[3072,3072]{1,0:T(8,128)(2,1)} %convolution_convert_fusion.3, bf16[3072,3072]{1,0:T(8,128)(2,1)} %get-tuple-element.123, bf16[6,32,3072]{2,1,0:T(8,128)(2,1)S(1)} %get-tuple-element.125, s32[]{:T(128)} %get-tuple-element.111, bf16[6,32,3072]{2,1,0:T(8,128)(2,1)S(1)} %get-tuple-element.122, ...), kind=kOutput, calls=%fused_computation.8.clone.1 | convolution fusion | flops 648120320 | bytes 38148096 | tf_op jit(solution)/shard_map/while/body/eval_jaxpr/dot_general | solution.py:36
  213.3 0.1 broadcast_in_dim.31
  213.4 0.1 dynamic_update_slice.5
  213.5 10.5 %psum.14 = f32[6,1024]{1,0:T(8,128)S(1)} all-reduce(f32[6,1024]{1,0:T(8,128)S(1)} %get-tuple-element.42), channel_id=1, replica_groups=mesh['pair'=2,'grow'=4,'gcol'=4] {'grow'}, use_global_device_ids=true, to_apply=%region_2.3 | all-reduce | flops 6144 | bytes 49152 | tf_op jit(solution)/shard_map/psum | solution.py:41
  224.0 17.3 %psum.15 = f32[6,1024]{1,0:T(8,128)S(1)} all-reduce(f32[6,1024]{1,0:T(8,128)S(1)} %psum.14), channel_id=1, replica_groups=mesh['pair'=2,'grow'=4,'gcol'=4] {'gcol'}, use_global_device_ids=true, to_apply=%region_3.4 | all-reduce | flops 6144 | bytes 49152 | tf_op jit(solution)/shard_map/psum | solution.py:41
  241.3 0.1 dynamic-slice_bitcast_fusion
  241.4 4.3 %all-gather = f32[2,6,64]{2,1,0:T(8,128)S(1)} all-gather(f32[1,6,64]{2,1,0:T(8,128)S(1)} %dynamic-slice_bitcast_fusion), channel_id=1, replica_groups=mesh['pair'=2,'grow'=4,'gcol'=4] {'pair'}, dimensions={0}, use_global_device_ids=true | all-gather | bytes 4608 | tf_op jit(solution)/shard_map/all_gather | solution.py:44
  245.8 0.6 gather_fusion
  246.3 0.7 broadcast_select_fusion
  (9 shorter events, 0.0 us)
Async XLA Ops:
  6.5 59.2 %all-gather.3.cloned.1.call-start = ((), (), s32[]{:S(2)}) async-start(), calls=%async_computation | async-start | bytes 5013504 | tf_op jit(solution)/shard_map/all_gather | solution.py:17
Sparse Core Ops, SparseCore 0:
  9.5 56.1 all-gather.2
